TPU v7x, 32 devices: a whole 2x2x4 slice. The times are simulated.
32 devices in a mesh: grp: 4 (over y, x), dev: 8 (over z, core).
Axes of the slice: x: 2, y: 2, z: 4, core: 2. Of those that a mesh axis runs over, the one named last changes fastest.
Arguments:
- points: float32 [64, 49152], P(None, 'dev'), may hold values from -6 to 6
- weights: float32 [49152, 128], P('dev'), may hold values from -4 to 4
- proj: float32 [256, 49152], P(None, 'dev'), may hold values from -0.078125 to 0.078125
- fetch_table: int32 [3, 8, 8, 2], P(None, 'dev'), may hold values from 0 to 11, as said below
- near_list: int32 [96, 16], P('dev'), may hold values from 0 to 15, as said below
- far_list: int32 [96, 8], P('dev'), may hold values from 0 to 7, as said below
- skel_idx: int32 [8, 256], P('dev'), may hold values from 0 to 6143, as said below
Outputs:
- potential: float32 [49152, 128], P('dev')
Inputs may be any that keep to these rules, and one draw needn't show every extreme that they name: Entries of fetch_table[r, d, e] are distinct local leaf numbers of column e. `near_list`: the 16 slots of one target leaf are distinct. `far_list`: the 8 nodes of one target leaf are distinct, and one of them is node (c + 1) mod 8 for the leaf's column c. `skel_idx`: the 256 skeleton points of one node are distinct.
All inputs are finite; a program needn't handle non-finite values.
Results may differ from a plain program's by a relative error of at most 0.0003.
Values sent between devices are 32-bit elements; how exact they have to be, the bound alone decides.
No kernel may reach another device: no remote copies, remote signals or barrier semaphores. Data moves between devices by JAX's collectives and lax.ppermute only.
A program may use at most 192 MiB of HBM per device.

v0:
```python
import jax
import jax.numpy as jnp
from jax import lax
from jax.sharding import PartitionSpec as P


def kernel_sum(target, sources, values):
    high = lax.Precision.HIGHEST
    inner = jnp.einsum("dt,jds->tjs", target, sources, precision=high)
    target_norm = jnp.sum(target * target, axis=0)
    source_norm = jnp.sum(sources * sources, axis=1)
    distance = target_norm[:, None, None] + source_norm[None] - 2.0 * inner
    kernel = jnp.exp(-distance * (2.0 / target.shape[0]))
    return jnp.einsum("tjs,jsw->tw", kernel, values, precision=high)


def on_device(points, weights, proj, fetch_table, near_list, far_list, skel_idx):
    features, column_points = points.shape
    columns = weights.shape[1]
    devices = lax.axis_size("dev")
    groups = lax.axis_size("grp")
    targets = near_list.shape[0]
    leaf_size = column_points // targets
    row_leaves = targets // (groups - 1)
    capacity = fetch_table.shape[3]
    group_index = lax.axis_index("grp")
    near_row = jnp.minimum(group_index, groups - 2)
    far_side = group_index == groups - 1
    leaf_coords = points.reshape(features, targets, leaf_size)
    leaf_weights = weights.reshape(targets, leaf_size, columns)
    requests = lax.dynamic_index_in_dim(fetch_table[:, 0], near_row, 0, keepdims=False)
    asked = lax.all_to_all(requests, "dev", split_axis=0, concat_axis=0, tiled=True)
    coords = jnp.moveaxis(jnp.take(leaf_coords, asked, axis=1), 0, 2)
    values = jnp.take(leaf_weights, asked, axis=0)
    fetched_coords = lax.all_to_all(coords, "dev", split_axis=0, concat_axis=0, tiled=True)
    fetched_values = lax.all_to_all(values, "dev", split_axis=0, concat_axis=0, tiled=True)
    flat_coords = fetched_coords.reshape(devices * capacity, features, leaf_size)
    flat_values = fetched_values.reshape(devices * capacity, leaf_size, columns)
    local_skeleton = jnp.take(points, skel_idx[0], axis=1)
    share_len = column_points // groups
    share_start = group_index * share_len
    share_proj = lax.dynamic_slice_in_dim(proj, share_start, share_len, 1)
    share_weights = lax.dynamic_slice_in_dim(weights, share_start, share_len, 0)
    partial_value = jnp.dot(
        share_proj,
        share_weights,
        preferred_element_type=jnp.float32,
        precision=lax.Precision.HIGHEST,
    )
    node_weights = lax.psum(partial_value, "grp")
    skel_coords, skel_weights = (
        lax.all_gather(local_skeleton[None], "dev", axis=0, tiled=True),
        lax.all_gather(node_weights[None], "dev", axis=0, tiled=True),
    )

    def near_work():
        slots = lax.dynamic_slice_in_dim(near_list, near_row * row_leaves, row_leaves, 0)
        leaf_numbers = near_row * row_leaves + jnp.arange(row_leaves, dtype=jnp.int32)

        def near_leaf(items):
            leaf_number, leaf_slots = items
            target = jnp.take(leaf_coords, leaf_number, axis=1)
            return kernel_sum(
                target,
                jnp.take(flat_coords, leaf_slots, axis=0),
                jnp.take(flat_values, leaf_slots, axis=0),
            )

        block = lax.map(near_leaf, (leaf_numbers, slots))
        empty = jnp.zeros((targets, leaf_size, columns), jnp.float32)
        return lax.dynamic_update_slice_in_dim(empty, block, near_row * row_leaves, 0)

    def far_work():

        def far_leaf(items):
            leaf_number, node_ids = items
            target = jnp.take(leaf_coords, leaf_number, axis=1)
            return kernel_sum(
                target,
                jnp.take(skel_coords, node_ids, axis=0),
                jnp.take(skel_weights, node_ids, axis=0),
            )

        return lax.map(far_leaf, (jnp.arange(targets, dtype=jnp.int32), far_list))

    contribution = lax.cond(far_side, far_work, near_work)
    total = lax.psum(contribution, "grp")
    return total.reshape(column_points, columns)


def solution(mesh):
    placed = (
        P(None, "dev"),
        P("dev", None),
        P(None, "dev"),
        P(None, "dev", None, None),
        P("dev", None),
        P("dev", None),
        P("dev", None),
    )
    return jax.shard_map(
        on_device, mesh=mesh, in_specs=placed, out_specs=P("dev", None), check_vma=False
    )
```

profile of v0, /device:TPU:0, one launch (start us, length us, event | category | flops | bytes accessed | tf_op | source)
XLA Modules:
  0.0 515.7 jit_solution(13828682134783458848)
XLA Ops:
  6.5 0.8 dynamic-slice_bitcast_fusion
  7.4 0.7 copy.24
  8.0 6.4 %all-to-all-start = ((s32[8,1,2]{2,1,0:T(1,128)}), s32[8,1,2]{2,1,0:T(1,128)S(1)}, u32[]{:S(2)}, u32[]{:S(2)}) async-start(s32[8,1,2]{2,1,0:T(1,128)} %copy.24), calls=%async_computation | async-start | bytes 8192 | tf_op jit(solution)/shard_map/all_to_all | solution.py:32
  14.4 2.7 copy.52
  17.1 2.8 all-to-all-done
  20.3 3.4 gather_fusion.4
  23.7 3.3 broadcast_select_fusion.1
  27.0 4.4 all-to-all-start.1
  31.4 2.8 gather_fusion.5
  34.2 4.6 broadcast_select_fusion
  38.8 41.6 %all-to-all-done.1 = f32[8,2,64,512]{3,2,1,0:T(8,128)} async-done(((f32[8,2,64,512]{3,2,1,0:T(8,128)}), f32[8,2,64,512]{3,2,1,0:T(8,128)}, u32[]{:S(2)}, u32[]{:S(2)}) %all-to-all-start.1) | async-done | bytes 2097184 | tf_op jit(solution)/shard_map/all_to_all | solution.py:35
  80.4 4.6 all-to-all-start.2
  85.0 3.5 fusion.72
  88.6 43.7 %all-reduce.3.cloned.1.call-done = f32[1,256,128]{2,1,0:T(8,128)} async-done(((f32[1,256,128]{2,1,0:T(8,128)}), f32[1,256,128]{2,1,0:T(8,128)}) %all-reduce.3.cloned.1.call-update) | async-done | bytes 131088 | tf_op jit(solution)/shard_map/psum | solution.py:50
  132.4 2.9 reshape.190
  135.2 2.3 copy.31
  137.5 2.6 gather_fusion.6
  140.3 56.1 %all_gather.6 = f32[8,64,256]{2,1,0:T(8,128)} all-gather(f32[1,64,256]{2,1,0:T(8,128)S(1)} %copy.32), channel_id=1, replica_groups=mesh['grp'=4,'dev'=8] {'dev'}, dimensions={0}, use_global_device_ids=true | all-gather | bytes 589824 | tf_op jit(solution)/shard_map/all_gather | solution.py:52
  196.5 202.2 %conditional.1 = (f32[12,512,128]{2,1,0:T(8,128)}) conditional(s32[]{:T(128)} %convert_element_type.3, (s32[]{:T(128)}, s32[12,16]{1,0:T(8,128)}, f32[8,2,64,512]{3,2,1,0:T(8,128)}, f32[8,2,512,128]{3,2,1,0:T(8,128)}, f32[64,12,512]{2,1,0:T(8,128)}) %tuple.20, (f32[64,12,512]{2,1,0:T(8,128)}, s32[12,8]{0,1:T(8,128)S(1)}, f32[8,64,256]{2,1,0:T(8,128)}, ...), branch_computations={%region_1.7_spmd, %region_6.12_spmd} | conditional | flops 9687917568 | bytes 60630836 | solution.py:86
  196.5 0.7 constant_dynamic-slice_fusion.2
  197.2 197.3 %while.19 = (s32[]{:T(128)}, f32[4,512,128]{2,1,0:T(8,128)}, s32[4]{0:T(128)S(1)}, f32[64,12,512]{2,1,0:T(8,128)}, s32[4,16]{1,0:T(4,128)S(1)}, /*index=5*/f32[1...) while((s32[]{:T(128)}, f32[4,512,128]{2,1,0:T(8,128)}, ...), condition=%wide.region_5.6_spmd, body=%wide.region_2.5_spmd.sunk | while | flops 9687917568 | bytes 55387260 | solution.py:69
  197.2 0.6 dynamic_slice.61
  199.7 1.3 constant_dynamic-slice_fusion.8
  201.1 2.3 gather_fusion.3
  203.4 16.2 %fusion.106 = f32[512,16,512]{2,0,1:T(8,128)} fusion(f32[16,64,512]{2,1,0:T(8,128)S(1)} %gather_fusion.3, pred[16]{0:T(512)(128)(4,1)S(1)} %compare_and_fusion.7, f32[64,1,512]{2,1,0:T(1,128)S(1)} %constant_dynamic-slice_fusion.8, pred[]{:T(512)S(6)} %and.56), kind=kOutput, calls=%fused_computation.22.clone.1 | convolution fusion | flops 3221782528 | bytes 19005456 | tf_op jit(solution)/shard_map/cond/branch_0_fun/while/body/eval_jaxpr/dt,jds->tjs/dot_general | solution.py:9
  220.0 5.0 gather_fusion.2
  225.0 21.5 %fusion.108 = f32[4,512,128]{2,1,0:T(8,128)} fusion(f32[4,512,128]{2,1,0:T(8,128)} %get-tuple-element.303, s32[]{:T(128)} %get-tuple-element.302, f32[16,512,128]{2,1,0:T(8,128)} %gather_fusion.2, pred[16]{0:T(512)(128)(4,1)S(1)} %compare_and_fusion.7, f32[512,16,512]{2,0,1:T(8,128)} %fusion.106, f32[16,512]{1,0:T(8,128)S(1)} %multiply_reduce_fusion.5, ...), kind=kOutput, calls=%fused_computation.25.clone.1 | convolution fusion | flops 6464471040 | bytes 21269008 | tf_op jit(solution)/shard_map/cond/branch_0_fun/while/body/eval_jaxpr/tjs,jsw->tw/dot_general | solution.py:14
  246.5 0.6 dynamic_slice.61
  249.0 1.3 constant_dynamic-slice_fusion.8
  250.4 2.3 gather_fusion.3
  252.7 16.2 %fusion.106 = f32[512,16,512]{2,0,1:T(8,128)} fusion(f32[16,64,512]{2,1,0:T(8,128)S(1)} %gather_fusion.3, pred[16]{0:T(512)(128)(4,1)S(1)} %compare_and_fusion.7, f32[64,1,512]{2,1,0:T(1,128)S(1)} %constant_dynamic-slice_fusion.8, pred[]{:T(512)S(6)} %and.56), kind=kOutput, calls=%fused_computation.22.clone.1 | convolution fusion | flops 3221782528 | bytes 19005456 | tf_op jit(solution)/shard_map/cond/branch_0_fun/while/body/eval_jaxpr/dt,jds->tjs/dot_general | solution.py:9
  269.3 5.0 gather_fusion.2
  274.3 21.5 %fusion.108 = f32[4,512,128]{2,1,0:T(8,128)} fusion(f32[4,512,128]{2,1,0:T(8,128)} %get-tuple-element.303, s32[]{:T(128)} %get-tuple-element.302, f32[16,512,128]{2,1,0:T(8,128)} %gather_fusion.2, pred[16]{0:T(512)(128)(4,1)S(1)} %compare_and_fusion.7, f32[512,16,512]{2,0,1:T(8,128)} %fusion.106, f32[16,512]{1,0:T(8,128)S(1)} %multiply_reduce_fusion.5, ...), kind=kOutput, calls=%fused_computation.25.clone.1 | convolution fusion | flops 6464471040 | bytes 21269008 | tf_op jit(solution)/shard_map/cond/branch_0_fun/while/body/eval_jaxpr/tjs,jsw->tw/dot_general | solution.py:14
  298.4 1.3 constant_dynamic-slice_fusion.8
  299.8 2.3 gather_fusion.3
  302.1 16.2 %fusion.106 = f32[512,16,512]{2,0,1:T(8,128)} fusion(f32[16,64,512]{2,1,0:T(8,128)S(1)} %gather_fusion.3, pred[16]{0:T(512)(128)(4,1)S(1)} %compare_and_fusion.7, f32[64,1,512]{2,1,0:T(1,128)S(1)} %constant_dynamic-slice_fusion.8, pred[]{:T(512)S(6)} %and.56), kind=kOutput, calls=%fused_computation.22.clone.1 | convolution fusion | flops 3221782528 | bytes 19005456 | tf_op jit(solution)/shard_map/cond/branch_0_fun/while/body/eval_jaxpr/dt,jds->tjs/dot_general | solution.py:9
  318.6 5.0 gather_fusion.2
  323.6 21.5 %fusion.108 = f32[4,512,128]{2,1,0:T(8,128)} fusion(f32[4,512,128]{2,1,0:T(8,128)} %get-tuple-element.303, s32[]{:T(128)} %get-tuple-element.302, f32[16,512,128]{2,1,0:T(8,128)} %gather_fusion.2, pred[16]{0:T(512)(128)(4,1)S(1)} %compare_and_fusion.7, f32[512,16,512]{2,0,1:T(8,128)} %fusion.106, f32[16,512]{1,0:T(8,128)S(1)} %multiply_reduce_fusion.5, ...), kind=kOutput, calls=%fused_computation.25.clone.1 | convolution fusion | flops 6464471040 | bytes 21269008 | tf_op jit(solution)/shard_map/cond/branch_0_fun/while/body/eval_jaxpr/tjs,jsw->tw/dot_general | solution.py:14
  345.1 0.6 dynamic_slice.61
  347.7 1.3 constant_dynamic-slice_fusion.8
  349.1 2.3 gather_fusion.3
  351.4 16.2 %fusion.106 = f32[512,16,512]{2,0,1:T(8,128)} fusion(f32[16,64,512]{2,1,0:T(8,128)S(1)} %gather_fusion.3, pred[16]{0:T(512)(128)(4,1)S(1)} %compare_and_fusion.7, f32[64,1,512]{2,1,0:T(1,128)S(1)} %constant_dynamic-slice_fusion.8, pred[]{:T(512)S(6)} %and.56), kind=kOutput, calls=%fused_computation.22.clone.1 | convolution fusion | flops 3221782528 | bytes 19005456 | tf_op jit(solution)/shard_map/cond/branch_0_fun/while/body/eval_jaxpr/dt,jds->tjs/dot_general | solution.py:9
  367.9 5.0 gather_fusion.2
  372.9 21.5 %fusion.108 = f32[4,512,128]{2,1,0:T(8,128)} fusion(f32[4,512,128]{2,1,0:T(8,128)} %get-tuple-element.303, s32[]{:T(128)} %get-tuple-element.302, f32[16,512,128]{2,1,0:T(8,128)} %gather_fusion.2, pred[16]{0:T(512)(128)(4,1)S(1)} %compare_and_fusion.7, f32[512,16,512]{2,0,1:T(8,128)} %fusion.106, f32[16,512]{1,0:T(8,128)S(1)} %multiply_reduce_fusion.5, ...), kind=kOutput, calls=%fused_computation.25.clone.1 | convolution fusion | flops 6464471040 | bytes 21269008 | tf_op jit(solution)/shard_map/cond/branch_0_fun/while/body/eval_jaxpr/tjs,jsw->tw/dot_general | solution.py:14
  394.5 2.0 broadcast.199
  396.4 2.3 constant_dynamic-update-slice_fusion
  398.7 106.7 %all-reduce.5.cloned.1.call-done = f32[6144,128]{1,0:T(8,128)} async-done(((f32[6144,128]{1,0:T(8,128)}), f32[6144,128]{1,0:T(8,128)}) %all-reduce.5.cloned.1.call-update) | async-done | bytes 3145744 | tf_op jit(solution)/shard_map/psum | solution.py:87
  505.4 3.8 copy.80
  (53 shorter events, 3.2 us)
Async XLA Ops:
  6.5 24.8 %copy-start = (f32[6144,128]{1,0:T(8,128)S(1)}, f32[6144,128]{1,0:T(8,128)}, u32[]{:S(2)}) copy-start(f32[6144,128]{1,0:T(8,128)} %param.16) | copy-start | bytes 9437188
  8.0 11.9 %all-to-all-start = ((s32[8,1,2]{2,1,0:T(1,128)}), s32[8,1,2]{2,1,0:T(1,128)S(1)}, u32[]{:S(2)}, u32[]{:S(2)}) async-start(s32[8,1,2]{2,1,0:T(1,128)} %copy.24), calls=%async_computation | async-start | bytes 8192 | tf_op jit(solution)/shard_map/all_to_all | solution.py:32
  27.0 53.4 %all-to-all-start.1 = ((f32[8,2,64,512]{3,2,1,0:T(8,128)}), f32[8,2,64,512]{3,2,1,0:T(8,128)}, u32[]{:S(2)}, u32[]{:S(2)}) async-start(f32[8,2,64,512]{3,2,1,0:T(8,128)} %broadcast_select_fusion.1), calls=%async_computation.1 | async-start | bytes 4194304 | tf_op jit(solution)/shard_map/all_to_all | solution.py:35
  80.4 116.1 %all-to-all-start.2 = ((f32[8,2,512,128]{3,2,1,0:T(8,128)}), f32[8,2,512,128]{3,2,1,0:T(8,128)}, u32[]{:S(2)}, u32[]{:S(2)}) async-start(f32[8,2,512,128]{3,2,1,0:T(8,128)} %broadcast_select_fusion), calls=%async_computation.2 | async-start | bytes 8388608 | tf_op jit(solution)/shard_map/all_to_all | solution.py:36
  85.0 47.3 %all-reduce.3.cloned.1.call-start = ((), (), s32[]{:S(2)}) async-start(), calls=%async_computation.3 | async-start | bytes 262144 | tf_op jit(solution)/shard_map/psum | solution.py:50
  88.5 46.7 %copy-start.3 = (f32[64,6144]{1,0:T(8,128)S(1)}, f32[64,6144]{1,0:T(8,128)}, u32[]{:S(2)}) copy-start(f32[64,6144]{1,0:T(8,128)} %param.15) | copy-start | bytes 4718596
  88.5 107.9 %all-gather.2.cloned.1.call-start = ((), (), s32[]{:S(2)}) async-start(), calls=%async_computation.4 | async-start | bytes 1179648 | tf_op jit(solution)/shard_map/all_gather | solution.py:53
  132.3 5.2 %copy-start.5 = (s32[1,256]{1,0:T(1,128)S(1)}, s32[1,256]{1,0:T(1,128)}, u32[]{:S(2)}) copy-start(s32[1,256]{1,0:T(1,128)} %param.21) | copy-start | bytes 3076
  132.3 64.1 %copy-start.4 = (s32[12,8]{0,1:T(8,128)S(1)}, s32[12,8]{0,1:T(8,128)}, u32[]{:S(2)}) copy-start(s32[12,8]{0,1:T(8,128)} %param.20) | copy-start | bytes 1156
  132.3 373.1 %all-reduce.5.cloned.1.call-start = ((), (), s32[]{:S(2)}) async-start(), calls=%async_computation.5 | async-start | bytes 6291456 | tf_op jit(solution)/shard_map/psum | solution.py:87
  398.7 110.5 %copy-start.1 = (f32[6144,128]{1,0:T(8,128)S(1)}, f32[6144,128]{1,0:T(8,128)}, u32[]{:S(2)}) copy-start(f32[6144,128]{1,0:T(8,128)} %param.16) | copy-start | bytes 9437188
Sparse Core Ops, SparseCore 0:
  88.7 43.5 all-reduce.2
  133.9 39.0 all-gather.1
  398.8 106.5 all-reduce.4
where the time goes:
time: 518 us; the launch traced here: 516 us
  waiting for transfers between devices  195 us (38%)
  matrix products  154 us (30%)
  local copies, waits for them, and re-layouts  64.2 us (12%)
  blocking collectives  56.1 us (11%)
  starting transfers between devices  15.4 us (3%)
  between operations  13.2 us (3%)
  other arithmetic  9.78 us (2%)
  loops' own time  7.83 us (2%)
    psum x1, waiting for transfers between devices, on_device(): total = lax.psum(contribution, 'grp')  107 us
    dot_general x4, matrix products, kernel_sum(): return jnp.einsum('tjs,jsw->tw', kernel, values, precision=high)  86.1 us
    dot_general x4, matrix products, kernel_sum(): inner = jnp.einsum('dt,jds->tjs', target, sources, precision=high)  64.6 us
    all_gather x1, blocking collectives, on_device(): lax.all_gather(local_skeleton[None], 'dev', axis=0, tiled=True)  56.1 us
    psum x1, waiting for transfers between devices, on_device(): node_weights = lax.psum(partial_value, 'grp')  43.7 us
    all_to_all x1, waiting for transfers between devices, on_device(): lax.all_to_all(coords, 'dev', split_axis=0, concat_axis=0, tiled=True)  41.6 us
    gather x4, local copies, waits for them, and re-layouts, near_leaf(): jnp.take(flat_values, leaf_slots, axis=0)  19.9 us
  transfers between devices with their start and end apart: 6, of which 4 were waited for; matrix products, arithmetic and copies ran while one was open for 4% of the time, Pallas kernels for 0%

commit v1 on v0

--- a/solution.py
+++ b/solution.py
@@ -84,7 +84,7 @@
         return lax.map(far_leaf, (jnp.arange(targets, dtype=jnp.int32), far_list))
 
     contribution = lax.cond(far_side, far_work, near_work)
-    total = lax.psum(contribution, "grp")
+    total = jnp.sum(lax.all_gather(contribution, "grp"), axis=0)
     return total.reshape(column_points, columns)
 
 

time: 518 us -> 557 us (1.075)
  waiting for transfers between devices: 195 us -> 230 us
  other arithmetic: 9.78 us -> 17.3 us
    all_gather x0 -> x1, waiting for transfers between devices: none -> 142 us  [on_device(): total = jnp.sum(lax.all_gather(contribution, 'grp'), axis=0)]
    psum x1 -> x0, waiting for transfers between devices: 107 us -> none  [on_device(): total = lax.psum(contribution, 'grp')]
    reduce_sum x0 -> x1, other arithmetic: none -> 7.56 us  [on_device(): total = jnp.sum(lax.all_gather(contribution, 'grp'), axis=0)]
where the time goes in v1:
time: 557 us; the launch traced here: 555 us
  waiting for transfers between devices  230 us (41%)
  matrix products  154 us (28%)
  local copies, waits for them, and re-layouts  60.5 us (11%)
  blocking collectives  56.1 us (10%)
  other arithmetic  17.3 us (3%)
  starting transfers between devices  15.4 us (3%)
  between operations  13.2 us (2%)
  loops' own time  7.83 us (1%)
    all_gather x1, waiting for transfers between devices, on_device(): total = jnp.sum(lax.all_gather(contribution, 'grp'), axis=0)  142 us
    dot_general x4, matrix products, kernel_sum(): return jnp.einsum('tjs,jsw->tw', kernel, values, precision=high)  86.1 us
    dot_general x4, matrix products, kernel_sum(): inner = jnp.einsum('dt,jds->tjs', target, sources, precision=high)  64.6 us
    all_gather x1, blocking collectives, on_device(): lax.all_gather(local_skeleton[None], 'dev', axis=0, tiled=True)  56.1 us
    psum x1, waiting for transfers between devices, on_device(): node_weights = lax.psum(partial_value, 'grp')  43.7 us
    all_to_all x1, waiting for transfers between devices, on_device(): lax.all_to_all(coords, 'dev', split_axis=0, concat_axis=0, tiled=True)  41.6 us
    gather x4, local copies, waits for them, and re-layouts, near_leaf(): jnp.take(flat_values, leaf_slots, axis=0)  19.9 us
  transfers between devices with their start and end apart: 6, of which 4 were waited for; matrix products, arithmetic and copies ran while one was open for 4% of the time, Pallas kernels for 0%

profile of v1, /device:TPU:0, one launch (start us, length us, event | category | flops | bytes accessed | tf_op | source)
XLA Modules:
  0.0 554.9 jit_solution(18411011494372701988)
XLA Ops:
  6.5 0.8 dynamic-slice_bitcast_fusion
  7.4 0.7 copy.24
  8.0 6.4 %all-to-all-start = ((s32[8,1,2]{2,1,0:T(1,128)}), s32[8,1,2]{2,1,0:T(1,128)S(1)}, u32[]{:S(2)}, u32[]{:S(2)}) async-start(s32[8,1,2]{2,1,0:T(1,128)} %copy.24), calls=%async_computation | async-start | bytes 8192 | tf_op jit(solution)/shard_map/all_to_all | solution.py:32
  14.4 2.7 copy.52
  17.1 2.8 all-to-all-done
  20.3 3.4 gather_fusion.4
  23.7 3.3 broadcast_select_fusion.1
  27.0 4.4 all-to-all-start.1
  31.4 2.8 gather_fusion.5
  34.2 4.6 broadcast_select_fusion
  38.8 41.6 %all-to-all-done.1 = f32[8,2,64,512]{3,2,1,0:T(8,128)} async-done(((f32[8,2,64,512]{3,2,1,0:T(8,128)}), f32[8,2,64,512]{3,2,1,0:T(8,128)}, u32[]{:S(2)}, u32[]{:S(2)}) %all-to-all-start.1) | async-done | bytes 2097184 | tf_op jit(solution)/shard_map/all_to_all | solution.py:35
  80.4 4.6 all-to-all-start.2
  85.0 3.5 fusion.72
  88.6 43.7 %all-reduce.2.cloned.1.call-done = f32[1,256,128]{2,1,0:T(8,128)} async-done(((f32[1,256,128]{2,1,0:T(8,128)}), f32[1,256,128]{2,1,0:T(8,128)}) %all-reduce.2.cloned.1.call-update) | async-done | bytes 131088 | tf_op jit(solution)/shard_map/psum | solution.py:50
  132.4 2.9 reshape.190
  135.2 2.3 copy.31
  137.5 2.6 gather_fusion.6
  140.3 56.1 %all_gather.12 = f32[8,64,256]{2,1,0:T(8,128)} all-gather(f32[1,64,256]{2,1,0:T(8,128)S(1)} %copy.32), channel_id=1, replica_groups=mesh['grp'=4,'dev'=8] {'dev'}, dimensions={0}, use_global_device_ids=true | all-gather | bytes 589824 | tf_op jit(solution)/shard_map/all_gather | solution.py:52
  196.5 202.2 %conditional.1 = (f32[12,512,128]{2,1,0:T(8,128)}) conditional(s32[]{:T(128)} %convert_element_type.3, (s32[]{:T(128)}, s32[12,16]{1,0:T(8,128)}, f32[8,2,64,512]{3,2,1,0:T(8,128)}, f32[8,2,512,128]{3,2,1,0:T(8,128)}, f32[64,12,512]{2,1,0:T(8,128)}) %tuple.20, (f32[64,12,512]{2,1,0:T(8,128)}, s32[12,8]{0,1:T(8,128)S(1)}, f32[8,64,256]{2,1,0:T(8,128)}, ...), branch_computations={%region_1.7_spmd, %region_6.12_spmd} | conditional | flops 9687917568 | bytes 60630836 | solution.py:86
  196.5 0.7 constant_dynamic-slice_fusion.2
  197.2 197.3 %while.19 = (s32[]{:T(128)}, f32[4,512,128]{2,1,0:T(8,128)}, s32[4]{0:T(128)S(1)}, f32[64,12,512]{2,1,0:T(8,128)}, s32[4,16]{1,0:T(4,128)S(1)}, /*index=5*/f32[1...) while((s32[]{:T(128)}, f32[4,512,128]{2,1,0:T(8,128)}, ...), condition=%wide.region_5.6_spmd, body=%wide.region_2.5_spmd.sunk | while | flops 9687917568 | bytes 55387260 | solution.py:69
  197.2 0.6 dynamic_slice.61
  199.7 1.3 constant_dynamic-slice_fusion.8
  201.1 2.3 gather_fusion.3
  203.4 16.2 %fusion.106 = f32[512,16,512]{2,0,1:T(8,128)} fusion(f32[16,64,512]{2,1,0:T(8,128)S(1)} %gather_fusion.3, pred[16]{0:T(512)(128)(4,1)S(1)} %compare_and_fusion.7, f32[64,1,512]{2,1,0:T(1,128)S(1)} %constant_dynamic-slice_fusion.8, pred[]{:T(512)S(6)} %and.56), kind=kOutput, calls=%fused_computation.22.clone.1 | convolution fusion | flops 3221782528 | bytes 19005456 | tf_op jit(solution)/shard_map/cond/branch_0_fun/while/body/eval_jaxpr/dt,jds->tjs/dot_general | solution.py:9
  220.0 5.0 gather_fusion.2
  225.0 21.5 %fusion.108 = f32[4,512,128]{2,1,0:T(8,128)} fusion(f32[4,512,128]{2,1,0:T(8,128)} %get-tuple-element.303, s32[]{:T(128)} %get-tuple-element.302, f32[16,512,128]{2,1,0:T(8,128)} %gather_fusion.2, pred[16]{0:T(512)(128)(4,1)S(1)} %compare_and_fusion.7, f32[512,16,512]{2,0,1:T(8,128)} %fusion.106, f32[16,512]{1,0:T(8,128)S(1)} %multiply_reduce_fusion.5, ...), kind=kOutput, calls=%fused_computation.25.clone.1 | convolution fusion | flops 6464471040 | bytes 21269008 | tf_op jit(solution)/shard_map/cond/branch_0_fun/while/body/eval_jaxpr/tjs,jsw->tw/dot_general | solution.py:14
  246.5 0.6 dynamic_slice.61
  249.0 1.3 constant_dynamic-slice_fusion.8
  250.4 2.3 gather_fusion.3
  252.7 16.2 %fusion.106 = f32[512,16,512]{2,0,1:T(8,128)} fusion(f32[16,64,512]{2,1,0:T(8,128)S(1)} %gather_fusion.3, pred[16]{0:T(512)(128)(4,1)S(1)} %compare_and_fusion.7, f32[64,1,512]{2,1,0:T(1,128)S(1)} %constant_dynamic-slice_fusion.8, pred[]{:T(512)S(6)} %and.56), kind=kOutput, calls=%fused_computation.22.clone.1 | convolution fusion | flops 3221782528 | bytes 19005456 | tf_op jit(solution)/shard_map/cond/branch_0_fun/while/body/eval_jaxpr/dt,jds->tjs/dot_general | solution.py:9
  269.3 5.0 gather_fusion.2
  274.3 21.5 %fusion.108 = f32[4,512,128]{2,1,0:T(8,128)} fusion(f32[4,512,128]{2,1,0:T(8,128)} %get-tuple-element.303, s32[]{:T(128)} %get-tuple-element.302, f32[16,512,128]{2,1,0:T(8,128)} %gather_fusion.2, pred[16]{0:T(512)(128)(4,1)S(1)} %compare_and_fusion.7, f32[512,16,512]{2,0,1:T(8,128)} %fusion.106, f32[16,512]{1,0:T(8,128)S(1)} %multiply_reduce_fusion.5, ...), kind=kOutput, calls=%fused_computation.25.clone.1 | convolution fusion | flops 6464471040 | bytes 21269008 | tf_op jit(solution)/shard_map/cond/branch_0_fun/while/body/eval_jaxpr/tjs,jsw->tw/dot_general | solution.py:14
  298.4 1.3 constant_dynamic-slice_fusion.8
  299.8 2.3 gather_fusion.3
  302.1 16.2 %fusion.106 = f32[512,16,512]{2,0,1:T(8,128)} fusion(f32[16,64,512]{2,1,0:T(8,128)S(1)} %gather_fusion.3, pred[16]{0:T(512)(128)(4,1)S(1)} %compare_and_fusion.7, f32[64,1,512]{2,1,0:T(1,128)S(1)} %constant_dynamic-slice_fusion.8, pred[]{:T(512)S(6)} %and.56), kind=kOutput, calls=%fused_computation.22.clone.1 | convolution fusion | flops 3221782528 | bytes 19005456 | tf_op jit(solution)/shard_map/cond/branch_0_fun/while/body/eval_jaxpr/dt,jds->tjs/dot_general | solution.py:9
  318.6 5.0 gather_fusion.2
  323.6 21.5 %fusion.108 = f32[4,512,128]{2,1,0:T(8,128)} fusion(f32[4,512,128]{2,1,0:T(8,128)} %get-tuple-element.303, s32[]{:T(128)} %get-tuple-element.302, f32[16,512,128]{2,1,0:T(8,128)} %gather_fusion.2, pred[16]{0:T(512)(128)(4,1)S(1)} %compare_and_fusion.7, f32[512,16,512]{2,0,1:T(8,128)} %fusion.106, f32[16,512]{1,0:T(8,128)S(1)} %multiply_reduce_fusion.5, ...), kind=kOutput, calls=%fused_computation.25.clone.1 | convolution fusion | flops 6464471040 | bytes 21269008 | tf_op jit(solution)/shard_map/cond/branch_0_fun/while/body/eval_jaxpr/tjs,jsw->tw/dot_general | solution.py:14
  345.1 0.6 dynamic_slice.61
  347.7 1.3 constant_dynamic-slice_fusion.8
  349.1 2.3 gather_fusion.3
  351.4 16.2 %fusion.106 = f32[512,16,512]{2,0,1:T(8,128)} fusion(f32[16,64,512]{2,1,0:T(8,128)S(1)} %gather_fusion.3, pred[16]{0:T(512)(128)(4,1)S(1)} %compare_and_fusion.7, f32[64,1,512]{2,1,0:T(1,128)S(1)} %constant_dynamic-slice_fusion.8, pred[]{:T(512)S(6)} %and.56), kind=kOutput, calls=%fused_computation.22.clone.1 | convolution fusion | flops 3221782528 | bytes 19005456 | tf_op jit(solution)/shard_map/cond/branch_0_fun/while/body/eval_jaxpr/dt,jds->tjs/dot_general | solution.py:9
  367.9 5.0 gather_fusion.2
  372.9 21.5 %fusion.108 = f32[4,512,128]{2,1,0:T(8,128)} fusion(f32[4,512,128]{2,1,0:T(8,128)} %get-tuple-element.303, s32[]{:T(128)} %get-tuple-element.302, f32[16,512,128]{2,1,0:T(8,128)} %gather_fusion.2, pred[16]{0:T(512)(128)(4,1)S(1)} %compare_and_fusion.7, f32[512,16,512]{2,0,1:T(8,128)} %fusion.106, f32[16,512]{1,0:T(8,128)S(1)} %multiply_reduce_fusion.5, ...), kind=kOutput, calls=%fused_computation.25.clone.1 | convolution fusion | flops 6464471040 | bytes 21269008 | tf_op jit(solution)/shard_map/cond/branch_0_fun/while/body/eval_jaxpr/tjs,jsw->tw/dot_general | solution.py:14
  394.5 2.0 broadcast.199
  396.4 2.3 constant_dynamic-update-slice_fusion
  398.7 142.1 %all-gather.6.cloned.1.call-done = f32[48,512,128]{2,1,0:T(8,128)} async-done(((f32[12,512,128]{2,1,0:T(8,128)}), f32[48,512,128]{2,1,0:T(8,128)}) %all-gather.6.cloned.1.call-update) | async-done | bytes 12582928 | tf_op jit(solution)/shard_map/all_gather | solution.py:87
  540.9 7.6 %reduce_sum.45 = f32[12,512,128]{2,1,0:T(8,128)} reduce(f32[4,12,512,128]{3,2,1,0:T(8,128)} %bitcast.98, f32[]{:T(128)} %constant.169.clone.1), dimensions={0}, to_apply=%region_11.13 | reduce | flops 2359296 | bytes 15728644 | tf_op jit(solution)/shard_map/reduce_sum | solution.py:87
  (53 shorter events, 3.2 us)
Async XLA Ops:
  6.5 24.8 %copy-start = (f32[6144,128]{1,0:T(8,128)S(1)}, f32[6144,128]{1,0:T(8,128)}, u32[]{:S(2)}) copy-start(f32[6144,128]{1,0:T(8,128)} %param.16) | copy-start | bytes 9437188
  8.0 11.9 %all-to-all-start = ((s32[8,1,2]{2,1,0:T(1,128)}), s32[8,1,2]{2,1,0:T(1,128)S(1)}, u32[]{:S(2)}, u32[]{:S(2)}) async-start(s32[8,1,2]{2,1,0:T(1,128)} %copy.24), calls=%async_computation | async-start | bytes 8192 | tf_op jit(solution)/shard_map/all_to_all | solution.py:32
  27.0 53.4 %all-to-all-start.1 = ((f32[8,2,64,512]{3,2,1,0:T(8,128)}), f32[8,2,64,512]{3,2,1,0:T(8,128)}, u32[]{:S(2)}, u32[]{:S(2)}) async-start(f32[8,2,64,512]{3,2,1,0:T(8,128)} %broadcast_select_fusion.1), calls=%async_computation.1 | async-start | bytes 4194304 | tf_op jit(solution)/shard_map/all_to_all | solution.py:35
  80.4 116.1 %all-to-all-start.2 = ((f32[8,2,512,128]{3,2,1,0:T(8,128)}), f32[8,2,512,128]{3,2,1,0:T(8,128)}, u32[]{:S(2)}, u32[]{:S(2)}) async-start(f32[8,2,512,128]{3,2,1,0:T(8,128)} %broadcast_select_fusion), calls=%async_computation.2 | async-start | bytes 8388608 | tf_op jit(solution)/shard_map/all_to_all | solution.py:36
  85.0 47.3 %all-reduce.2.cloned.1.call-start = ((), (), s32[]{:S(2)}) async-start(), calls=%async_computation.3 | async-start | bytes 262144 | tf_op jit(solution)/shard_map/psum | solution.py:50
  88.5 46.7 %copy-start.3 = (f32[64,6144]{1,0:T(8,128)S(1)}, f32[64,6144]{1,0:T(8,128)}, u32[]{:S(2)}) copy-start(f32[64,6144]{1,0:T(8,128)} %param.15) | copy-start | bytes 4718596
  88.5 107.9 %all-gather.4.cloned.1.call-start = ((), (), s32[]{:S(2)}) async-start(), calls=%async_computation.4 | async-start | bytes 1179648 | tf_op jit(solution)/shard_map/all_gather | solution.py:53
  132.3 5.2 copy-start.5
  132.3 64.1 %copy-start.4 = (s32[12,8]{0,1:T(8,128)S(1)}, s32[12,8]{0,1:T(8,128)}, u32[]{:S(2)}) copy-start(s32[12,8]{0,1:T(8,128)} %param.20) | copy-start | bytes 1156
  132.3 408.5 %all-gather.6.cloned.1.call-start = ((), (), s32[]{:S(2)}) async-start(), calls=%async_computation.5 | async-start | bytes 15728640 | tf_op jit(solution)/shard_map/all_gather | solution.py:87
  540.9 7.6 %copy-start.1 = (f32[6144,128]{1,0:T(8,128)S(1)}, f32[6144,128]{1,0:T(8,128)}, u32[]{:S(2)}) copy-start(f32[6144,128]{1,0:T(8,128)} %param.16) | copy-start | bytes 9437188
Sparse Core Ops, SparseCore 0:
  88.7 43.5 all-reduce.1
  133.9 39.0 all-gather.3
  398.8 141.9 all-gather.5
